TPU v7x, 128 devices: a whole 4x4x4 slice. The times are simulated.
128 devices in a mesh: seq: 32 (over z, y, core), tp: 4 (over x).
Axes of the slice: x: 4, y: 4, z: 4, core: 2. Of those that a mesh axis runs over, the one named last changes fastest.
Arguments:
- states: bfloat16 [256, 3072], P(None, 'seq'), may hold values from -20 to 20
- norm_gain: bfloat16 [3072], P('seq'), may hold values from 0.25 to 1.75
- w_qkv: bfloat16 [3, 3072, 3072], P(None, 'seq', 'tp'), may hold values from -0.109375 to 0.109375
- w_out: bfloat16 [3072, 3072], P('tp', 'seq'), may hold values from -0.109375 to 0.109375
- cache: bfloat16 [768, 2, 64, 3072], P('seq', None, None, 'tp'), may hold values from -400 to 400
- context_len: int32 [256], replicated, may hold values from 1 to 4096, as said below
- block_owner: int32 [768], P('seq'), may hold values from 0 to 256, as said below
- block_index: int32 [768], P('seq'), may hold values from 0 to 63, as said below
Outputs:
- hidden: bfloat16 [256, 3072], P('tp', 'seq')
- updated: bfloat16 [768, 2, 64, 3072], P('seq', None, None, 'tp')
Inputs may be any that keep to these rules, and one draw needn't show every extreme that they name: `context_len`: A request of length n owns exactly ceil(n / 64) pool blocks, with block_index 0, 1, ... once each; at least one pool block is unused. `context_len`: exactly 4 requests own 64/2 blocks or more; every other request owns at most 2 blocks, all on one index of seq. `block_owner`: the value 256 marks an unused block. `block_index`: 0 for an unused block.
All inputs are finite; a program needn't handle non-finite values.
Results may differ from a plain program's by a relative error of at most 0.0068.
Values may be sent and summed in bfloat16 or wider, within the bound.
A program may use at most 128 MiB of HBM per device.

v0:
```python
import jax
import jax.numpy as jnp
from jax import lax
from jax.sharding import PartitionSpec as P

HEAD_DIM = 96
EPSILON = 1e-05
NEG_FLOOR = -1e30


def combined_all(part, axis, combine):
    gathered = jax.tree.map(lambda a: lax.all_gather(a, axis), part)

    def take(source):
        return jax.tree.map(lambda a: lax.dynamic_index_in_dim(a, source, 0, False), gathered)

    return lax.fori_loop(
        1, lax.axis_size(axis), lambda source, state: combine(state, take(source)), take(0)
    )


def rotate(values, positions):
    half_dim = HEAD_DIM // 2
    frequency = 10000.0 ** (-jnp.arange(half_dim, dtype=jnp.float32) * 2.0 / HEAD_DIM)
    angles = positions.astype(jnp.float32)[:, None] * frequency[None, :]
    cosine = jnp.cos(angles)[:, None, :]
    sine_part = jnp.sin(angles)[:, None, :]
    front_half = values[..., :half_dim]
    back_half = values[..., half_dim:]
    return jnp.concatenate(
        [front_half * cosine - back_half * sine_part, back_half * cosine + front_half * sine_part],
        axis=-1,
    )


def finish(projected, positions):
    row_count = projected.shape[0]
    columns = projected.shape[2]
    head_count = columns // HEAD_DIM
    query = rotate(
        projected[:, 0].reshape(row_count, head_count, HEAD_DIM), positions
    ) * HEAD_DIM ** (-0.5)
    keys_new = rotate(projected[:, 1].reshape(row_count, head_count, HEAD_DIM), positions)
    return (
        query.astype(jnp.bfloat16).reshape(row_count, columns),
        keys_new.astype(jnp.bfloat16).reshape(row_count, columns),
        projected[:, 2].astype(jnp.bfloat16),
    )


def join(earlier, later):
    highest = jnp.maximum(earlier[0], later[0])
    left_scale = jnp.exp(earlier[0] - highest)
    right_scale = jnp.exp(later[0] - highest)
    return (
        highest,
        earlier[1] * left_scale + later[1] * right_scale,
        earlier[2] * jnp.repeat(left_scale, HEAD_DIM, axis=1)
        + later[2] * jnp.repeat(right_scale, HEAD_DIM, axis=1),
    )


def shards(states, norm_gain, w_qkv, w_out, cache, context_len, block_owner, block_index):
    requests = states.shape[0]
    seq_count = lax.axis_size("seq")
    wide_states = states.astype(jnp.float32)
    sum_squares = lax.psum(jnp.sum(wide_states * wide_states, axis=1), "seq")
    inverse = lax.rsqrt(sum_squares / (states.shape[1] * seq_count) + EPSILON)
    normed = (wide_states * inverse[:, None] * norm_gain.astype(jnp.float32)[None, :]).astype(
        jnp.bfloat16
    )
    positions = context_len - 1
    local_term = jnp.einsum("rd,cdh->rch", normed, w_qkv, preferred_element_type=jnp.float32)
    projected = lax.psum(local_term, "seq")
    query, keys_new, values_new = finish(projected, positions)
    blocks, _, tokens, columns = cache.shape
    head_count = columns // HEAD_DIM
    block_live = block_owner < requests
    owner_row = jnp.minimum(block_owner, requests - 1)
    last_position = positions[owner_row]
    block_hit = block_live & (block_index == last_position // tokens)
    slot_hit = block_hit[:, None] & (
        jnp.arange(tokens, dtype=jnp.int32)[None, :] == (last_position % tokens)[:, None]
    )
    fresh_rows = jnp.stack([keys_new[owner_row], values_new[owner_row]], axis=1)
    updated = jnp.where(slot_hit[:, None, :, None], fresh_rows[:, :, None, :], cache)
    query_rows = query[owner_row].reshape(blocks, head_count, HEAD_DIM)
    key_cache = updated[:, 0].reshape(blocks, tokens, head_count, HEAD_DIM)
    value_cache = updated[:, 1].reshape(blocks, tokens, head_count, HEAD_DIM)
    scores = jnp.einsum("bhd,bthd->bht", query_rows, key_cache, preferred_element_type=jnp.float32)
    token_position = block_index[:, None] * tokens + jnp.arange(tokens, dtype=jnp.int32)[None, :]
    visible = block_live[:, None] & (token_position < context_len[owner_row][:, None])
    masked = jnp.where(visible[:, None, :], scores, NEG_FLOOR)
    block_max = jnp.max(masked, axis=-1)
    weights = jnp.where(visible[:, None, :], jnp.exp(masked - block_max[..., None]), 0.0).astype(
        jnp.bfloat16
    )
    block_sum = jnp.sum(weights.astype(jnp.float32), axis=-1)
    block_out = jnp.einsum(
        "bht,bthd->bhd", weights, value_cache, preferred_element_type=jnp.float32
    ).reshape(blocks, columns)
    segment = jnp.where(block_live, block_owner, requests)
    member = segment[None, :] == jnp.arange(requests, dtype=jnp.int32)[:, None]
    local_max = jnp.max(jnp.where(member[:, :, None], block_max[None, :, :], NEG_FLOOR), axis=1)
    factor = jnp.exp(block_max - local_max[owner_row])
    member_matrix = member.astype(jnp.float32)
    totals = jnp.dot(member_matrix, block_sum * factor, precision=lax.Precision.HIGHEST)
    outputs = jnp.dot(
        member_matrix,
        block_out * jnp.repeat(factor, HEAD_DIM, axis=1),
        precision=lax.Precision.HIGHEST,
    )
    merged = combined_all((local_max, totals, outputs), "seq", join)
    attended = (merged[2] / jnp.repeat(merged[1], HEAD_DIM, axis=1)).astype(jnp.bfloat16)
    terms = jnp.dot(attended, w_out, preferred_element_type=jnp.float32)
    summed = lax.psum_scatter(terms, "tp", scatter_dimension=0, tiled=True)
    row_count = summed.shape[0]
    residual_rows = lax.dynamic_slice_in_dim(
        wide_states, lax.axis_index("tp") * row_count, row_count, 0
    )
    hidden = (summed + residual_rows).astype(jnp.bfloat16)
    return (hidden, updated)


def solution(mesh):
    return jax.shard_map(
        shards,
        mesh=mesh,
        in_specs=(
            P(None, "seq"),
            P("seq"),
            P(None, "seq", "tp"),
            P("tp", "seq"),
            P("seq", None, None, "tp"),
            P(),
            P("seq"),
            P("seq"),
        ),
        out_specs=(P("tp", "seq"), P("seq", None, None, "tp")),
        check_vma=False,
    )
```

profile of v0, /device:TPU:0, one launch (start us, length us, event | category | flops | bytes accessed | tf_op | source)
XLA Modules:
  0.0 399.5 jit_solution(8305740966183515385)
XLA Ops:
  8.1 68.7 %psum.14 = f32[256]{0:T(256)S(1)} all-reduce(f32[256]{0:T(256)S(1)} %multiply_reduce_fusion), channel_id=1, replica_groups=mesh['seq'=32,'tp'=4] {'seq'}, use_global_device_ids=true, to_apply=%region_1.0 | all-reduce | flops 256 | bytes 2048 | tf_op jit(solution)/shard_map/psum | solution.py:67
  77.5 2.8 fusion.12
  82.3 102.0 %all-reduce.2.cloned.1.call-done = f32[256,3,768]{2,0,1:T(8,128)} async-done(((f32[256,3,768]{2,0,1:T(8,128)}), f32[256,3,768]{2,0,1:T(8,128)}) %all-reduce.2.cloned.1.call-update) | async-done | bytes 2359312 | tf_op jit(solution)/shard_map/psum | solution.py:74
  184.3 1.5 fusion.28
  190.1 2.7 broadcast_select_fusion
  192.8 2.2 fusion.27
  195.7 6.4 %reshape_squeeze.14 = bf16[24,64,8,96]{3,2,1,0:T(8,128)(2,1)} reshape(bf16[24,1,64,768]{3,2,1,0:T(8,128)(2,1)} %get-tuple-element.239) | data formatting | bytes 4718592 | tf_op jit(solution)/shard_map/reshape;squeeze | solution.py:88
  204.3 1.7 gather_fusion.1
  206.1 3.6 fusion.5
  210.0 4.3 %reshape_squeeze.15 = bf16[24,64,8,96]{3,2,1,0:T(8,128)(2,1)} reshape(bf16[24,1,64,768]{3,2,1,0:T(8,128)(2,1)S(1)} %get-tuple-element.238) | data formatting | bytes 4718592 | tf_op jit(solution)/shard_map/reshape;squeeze | solution.py:89
  215.1 2.8 fusion.3
  218.1 1.5 fusion.17
  219.9 25.3 %all-gather.1 = f32[8192,8]{0,1:T(8,128)S(1)} all-gather(f32[256,8]{0,1:T(8,128)S(1)} %fusion.18), channel_id=3, replica_groups=mesh['seq'=32,'tp'=4] {'seq'}, dimensions={0}, use_global_device_ids=true | all-gather | bytes 270336 | tf_op jit(solution)/shard_map/all_gather | solution.py:12
  245.2 22.3 %all-gather = f32[8192,8]{0,1:T(8,128)S(1)} all-gather(f32[256,8]{0,1:T(8,128)S(1)} %select_reduce_fusion), channel_id=2, replica_groups=mesh['seq'=32,'tp'=4] {'seq'}, dimensions={0}, use_global_device_ids=true | all-gather | bytes 270336 | tf_op jit(solution)/shard_map/all_gather | solution.py:12
  267.5 44.9 %all-gather.5.cloned.1.call-done = f32[8192,768]{1,0:T(8,128)} async-done(((f32[256,768]{1,0:T(8,128)}), f32[8192,768]{1,0:T(8,128)}) %all-gather.5.cloned.1.call-update) | async-done | bytes 25165840 | tf_op jit(solution)/shard_map/all_gather | solution.py:12
  313.9 56.6 %while.19 = (s32[]{:T(128)}, f32[256,8]{0,1:T(8,128)S(1)}, f32[256,8]{0,1:T(8,128)S(1)}, f32[256,768]{0,1:T(8,128)S(1)}, f32[32,256,8]{1,2,0:T(8,128)S(1)}, /*in...) while((s32[]{:T(128)}, f32[256,8]{0,1:T(8,128)S(1)}, ...), condition=%wide.region_7.8_spmd, body=%wide.region_6.7_spmd.sunk | while | flops 602117 | bytes 5587095 | solution.py:17
  314.0 1.2 constant_dynamic-slice_fusion.2
  317.7 1.2 constant_dynamic-slice_fusion.2
  321.3 1.2 constant_dynamic-slice_fusion.2
  325.0 1.2 constant_dynamic-slice_fusion.2
  328.6 1.2 constant_dynamic-slice_fusion.2
  332.2 1.2 constant_dynamic-slice_fusion.2
  334.1 1.2 constant_dynamic-slice_fusion.2
  371.6 19.7 %reduce-scatter.4.cloned.1.call-done = f32[64,96]{1,0:T(8,128)} async-done(((f32[256,96]{1,0:T(8,128)}), f32[64,96]{1,0:T(8,128)}) %reduce-scatter.4.cloned.1.call-update) | async-done | bytes 24592
  (184 shorter events, 63.4 us)
Async XLA Ops:
  7.2 70.3 %copy-start = (bf16[3,96,768]{2,1,0:T(8,128)(2,1)S(1)}, bf16[3,96,768]{2,1,0:T(8,128)(2,1)}, u32[]{:S(2)}) copy-start(bf16[3,96,768]{2,1,0:T(8,128)(2,1)} %param.12) | copy-start | bytes 1327108
  7.2 73.1 %copy-start.1 = (s32[256]{0:T(256)S(1)}, s32[256]{0:T(256)}, u32[]{:S(2)}) copy-start(s32[256]{0:T(256)} %param.15) | copy-start | bytes 3076
  7.2 73.1 %copy-start.5 = (s32[24]{0:T(128)S(1)}, s32[24]{0:T(128)}, u32[]{:S(2)}) copy-start(s32[24]{0:T(128)} %param.16) | copy-start | bytes 292
  7.2 177.1 %all-reduce.2.cloned.1.call-start = ((), (), s32[]{:S(2)}) async-start(), calls=%async_computation.1 | async-start | bytes 4718592 | tf_op jit(solution)/shard_map/psum | solution.py:74
  8.1 73.7 %copy-start.6 = (s32[24]{0:T(128)S(1)}, s32[24]{0:T(128)}, u32[]{:S(2)}) copy-start(s32[24]{0:T(128)} %param.17) | copy-start | bytes 292
  80.3 232.2 %all-gather.5.cloned.1.call-start = ((), (), s32[]{:S(2)}) async-start(), calls=%async_computation.2 | async-start | bytes 25952256 | tf_op jit(solution)/shard_map/all_gather | solution.py:12
  192.8 2.9 copy-start.2
  219.7 171.6 %reduce-scatter.4.cloned.1.call-start = ((), (), s32[]{:S(2)}) async-start(), calls=%async_computation.3 | async-start | bytes 163840
  313.9 56.7 %copy-start.4 = (bf16[768,96]{0,1:T(8,128)(2,1)S(1)}, bf16[768,96]{0,1:T(8,128)(2,1)}, u32[]{:S(2)}) copy-start(bf16[768,96]{0,1:T(8,128)(2,1)} %param.13) | copy-start | bytes 442372
  313.9 57.7 %copy-start.3 = (bf16[256,96]{0,1:T(8,128)(2,1)S(1)}, bf16[256,96]{0,1:T(8,128)(2,1)}, u32[]{:S(2)}) copy-start(bf16[256,96]{0,1:T(8,128)(2,1)} %param.10) | copy-start | bytes 147460
Sparse Core Ops, SparseCore 0:
  80.4 103.8 all-reduce.1
  219.8 92.5 all-gather.4
  371.7 19.5 reduce-scatter.3
where the time goes:
time: 402 us; the launch traced here: 399 us
  waiting for transfers between devices  167 us (42%)
  blocking collectives  116 us (29%)
  local copies, waits for them, and re-layouts  71.3 us (18%)
  other arithmetic  18 us (4%)
  between operations  14.1 us (4%)
  matrix products  11.8 us (3%)
    psum x1, waiting for transfers between devices, shards(): projected = lax.psum(local_term, 'seq')  102 us
    psum x1, blocking collectives, shards(): sum_squares = lax.psum(jnp.sum(wide_states * wide_states, axis=1), 'seq')  68.7 us
    all_gather x2, blocking collectives, combined_all(): gathered = jax.tree.map(lambda a: lax.all_gather(a, axis), part)  47.6 us
    dynamic_slice x65, local copies, waits for them, and re-layouts, take(): lax.dynamic_index_in_dim(a, source, 0, False)  46.3 us
    all_gather x1, waiting for transfers between devices, combined_all(): gathered = jax.tree.map(lambda a: lax.all_gather(a, axis), part)  44.9 us
    unnamed x4, waiting for transfers between devices  19.8 us
    add x31, other arithmetic, join(): earlier[2] * jnp.repeat(left_scale, HEAD_DIM, axis=1)  9.66 us
  transfers between devices with their start and end apart: 3, of which 3 were waited for; matrix products, arithmetic and copies ran while one was open for 1% of the time, Pallas kernels for 0%

commit v1 on v0

--- a/solution.py
+++ b/solution.py
@@ -64,7 +64,9 @@
     requests = states.shape[0]
     seq_count = lax.axis_size("seq")
     wide_states = states.astype(jnp.float32)
-    sum_squares = lax.psum(jnp.sum(wide_states * wide_states, axis=1), "seq")
+    own = jnp.sum(wide_states * wide_states, axis=1)
+    terms_2 = lax.all_gather(own, "seq")
+    sum_squares = jnp.sum(terms_2, axis=0)
     inverse = lax.rsqrt(sum_squares / (states.shape[1] * seq_count) + EPSILON)
     normed = (wide_states * inverse[:, None] * norm_gain.astype(jnp.float32)[None, :]).astype(
         jnp.bfloat16

time: 402 us -> 361 us (0.90)
  blocking collectives: 116 us -> 73.3 us
    psum x1 -> x0, blocking collectives: 68.7 us -> none  [shards(): sum_squares = lax.psum(jnp.sum(wide_states * wide_states, axis=1), 'seq')]
    all_gather x0 -> x1, blocking collectives: none -> 25.7 us  [shards(): terms_2 = lax.all_gather(own, 'seq')]
where the time goes in v1:
time: 361 us; the launch traced here: 359 us
  waiting for transfers between devices  170 us (47%)
  blocking collectives  73.3 us (20%)
  local copies, waits for them, and re-layouts  71.3 us (20%)
  other arithmetic  18 us (5%)
  between operations  14.1 us (4%)
  matrix products  11.8 us (3%)
    psum x1, waiting for transfers between devices, shards(): projected = lax.psum(local_term, 'seq')  105 us
    all_gather x2, blocking collectives, combined_all(): gathered = jax.tree.map(lambda a: lax.all_gather(a, axis), part)  47.6 us
    dynamic_slice x65, local copies, waits for them, and re-layouts, take(): lax.dynamic_index_in_dim(a, source, 0, False)  46.3 us
    all_gather x1, waiting for transfers between devices, combined_all(): gathered = jax.tree.map(lambda a: lax.all_gather(a, axis), part)  44.9 us
    all_gather x1, blocking collectives, shards(): terms_2 = lax.all_gather(own, 'seq')  25.7 us
    unnamed x4, waiting for transfers between devices  19.7 us
    add x31, other arithmetic, join(): earlier[2] * jnp.repeat(left_scale, HEAD_DIM, axis=1)  9.66 us
  transfers between devices with their start and end apart: 3, of which 3 were waited for; matrix products, arithmetic and copies ran while one was open for 1% of the time, Pallas kernels for 0%

profile of v1, /device:TPU:0, one launch (start us, length us, event | category | flops | bytes accessed | tf_op | source)
XLA Modules:
  0.0 359.5 jit_solution(6453313781373265771)
XLA Ops:
  8.1 25.7 %all-gather.4 = f32[32,1,256]{2,1,0:T(1,128)S(1)} all-gather(f32[1,1,256]{2,1,0:T(1,128)S(1)} %bitcast.76), channel_id=2, replica_groups=mesh['seq'=32,'tp'=4] {'seq'}, dimensions={0}, use_global_device_ids=true | all-gather | bytes 33792 | tf_op jit(solution)/shard_map/all_gather | solution.py:68
  34.6 2.8 fusion.12
  39.4 104.9 %all-reduce.2.cloned.1.call-done = f32[256,3,768]{2,0,1:T(8,128)} async-done(((f32[256,3,768]{2,0,1:T(8,128)}), f32[256,3,768]{2,0,1:T(8,128)}) %all-reduce.2.cloned.1.call-update) | async-done | bytes 2359312 | tf_op jit(solution)/shard_map/psum | solution.py:76
  144.3 1.5 fusion.28
  150.1 2.7 broadcast_select_fusion
  152.8 2.2 fusion.27
  155.7 6.4 %reshape_squeeze.14 = bf16[24,64,8,96]{3,2,1,0:T(8,128)(2,1)} reshape(bf16[24,1,64,768]{3,2,1,0:T(8,128)(2,1)} %get-tuple-element.246) | data formatting | bytes 4718592 | tf_op jit(solution)/shard_map/reshape;squeeze | solution.py:90
  164.3 1.7 gather_fusion.1
  166.1 3.6 %fusion.5 = f32[24,8,1,64]{3,2,1,0:T(1,128)S(1)} fusion(bf16[24,8,96,1]{2,3,1,0:T(2,128)(2,1)S(1)} %reshape.285, bf16[24,64,8,96]{3,2,1,0:T(8,128)(2,1)} %reshape_squeeze.14), kind=kOutput, calls=%fused_computation.19 | convolution fusion | flops 2359296 | bytes 2445312 | tf_op jit(solution)/shard_map/bhd,bthd->bht/dot_general | solution.py:92
  170.0 4.3 %reshape_squeeze.15 = bf16[24,64,8,96]{3,2,1,0:T(8,128)(2,1)} reshape(bf16[24,1,64,768]{3,2,1,0:T(8,128)(2,1)S(1)} %get-tuple-element.245) | data formatting | bytes 4718592 | tf_op jit(solution)/shard_map/reshape;squeeze | solution.py:91
  175.1 2.8 fusion.3
  178.1 1.5 fusion.17
  179.9 25.3 %all-gather.2 = f32[8192,8]{0,1:T(8,128)S(1)} all-gather(f32[256,8]{0,1:T(8,128)S(1)} %fusion.18), channel_id=4, replica_groups=mesh['seq'=32,'tp'=4] {'seq'}, dimensions={0}, use_global_device_ids=true | all-gather | bytes 270336 | tf_op jit(solution)/shard_map/all_gather | solution.py:12
  205.2 22.3 %all-gather.1 = f32[8192,8]{0,1:T(8,128)S(1)} all-gather(f32[256,8]{0,1:T(8,128)S(1)} %select_reduce_fusion), channel_id=3, replica_groups=mesh['seq'=32,'tp'=4] {'seq'}, dimensions={0}, use_global_device_ids=true | all-gather | bytes 270336 | tf_op jit(solution)/shard_map/all_gather | solution.py:12
  227.5 44.9 %all-gather.7.cloned.1.call-done = f32[8192,768]{1,0:T(8,128)} async-done(((f32[256,768]{1,0:T(8,128)}), f32[8192,768]{1,0:T(8,128)}) %all-gather.7.cloned.1.call-update) | async-done | bytes 25165840 | tf_op jit(solution)/shard_map/all_gather | solution.py:12
  273.9 56.6 %while.19 = (s32[]{:T(128)}, f32[256,8]{0,1:T(8,128)S(1)}, f32[256,8]{0,1:T(8,128)S(1)}, f32[256,768]{0,1:T(8,128)S(1)}, f32[32,256,8]{1,2,0:T(8,128)S(1)}, /*in...) while((s32[]{:T(128)}, f32[256,8]{0,1:T(8,128)S(1)}, ...), condition=%wide.region_7.8_spmd, body=%wide.region_6.7_spmd.sunk | while | flops 602117 | bytes 5587095 | solution.py:17
  274.0 1.2 constant_dynamic-slice_fusion.2
  275.8 1.2 constant_dynamic-slice_fusion.2
  277.7 1.2 constant_dynamic-slice_fusion.2
  281.3 1.2 constant_dynamic-slice_fusion.2
  284.9 1.2 constant_dynamic-slice_fusion.2
  288.6 1.2 constant_dynamic-slice_fusion.2
  292.2 1.2 constant_dynamic-slice_fusion.2
  331.6 19.7 %reduce-scatter.4.cloned.1.call-done = f32[64,96]{1,0:T(8,128)} async-done(((f32[256,96]{1,0:T(8,128)}), f32[64,96]{1,0:T(8,128)}) %reduce-scatter.4.cloned.1.call-update) | async-done | bytes 24592
  (185 shorter events, 63.5 us)
Async XLA Ops:
  7.2 27.4 %copy-start = (bf16[3,96,768]{2,1,0:T(8,128)(2,1)S(1)}, bf16[3,96,768]{2,1,0:T(8,128)(2,1)}, u32[]{:S(2)}) copy-start(bf16[3,96,768]{2,1,0:T(8,128)(2,1)} %param.12) | copy-start | bytes 1327108
  7.2 30.2 %copy-start.1 = (s32[256]{0:T(256)S(1)}, s32[256]{0:T(256)}, u32[]{:S(2)}) copy-start(s32[256]{0:T(256)} %param.15) | copy-start | bytes 3076
  7.2 30.3 %copy-start.5 = (s32[24]{0:T(128)S(1)}, s32[24]{0:T(128)}, u32[]{:S(2)}) copy-start(s32[24]{0:T(128)} %param.16) | copy-start | bytes 292
  7.2 137.1 %all-reduce.2.cloned.1.call-start = ((), (), s32[]{:S(2)}) async-start(), calls=%async_computation.1 | async-start | bytes 4718592 | tf_op jit(solution)/shard_map/psum | solution.py:76
  33.9 5.0 %copy-start.6 = (s32[24]{0:T(128)S(1)}, s32[24]{0:T(128)}, u32[]{:S(2)}) copy-start(s32[24]{0:T(128)} %param.17) | copy-start | bytes 292
  37.4 235.1 %all-gather.7.cloned.1.call-start = ((), (), s32[]{:S(2)}) async-start(), calls=%async_computation.2 | async-start | bytes 25952256 | tf_op jit(solution)/shard_map/all_gather | solution.py:12
  152.8 2.9 copy-start.2
  179.7 171.6 %reduce-scatter.4.cloned.1.call-start = ((), (), s32[]{:S(2)}) async-start(), calls=%async_computation.3 | async-start | bytes 163840
  273.9 56.7 %copy-start.4 = (bf16[768,96]{0,1:T(8,128)(2,1)S(1)}, bf16[768,96]{0,1:T(8,128)(2,1)}, u32[]{:S(2)}) copy-start(bf16[768,96]{0,1:T(8,128)(2,1)} %param.13) | copy-start | bytes 442372
  273.9 57.7 %copy-start.3 = (bf16[256,96]{0,1:T(8,128)(2,1)S(1)}, bf16[256,96]{0,1:T(8,128)(2,1)}, u32[]{:S(2)}) copy-start(bf16[256,96]{0,1:T(8,128)(2,1)} %param.10) | copy-start | bytes 147460
Sparse Core Ops, SparseCore 0:
  37.5 106.7 all-reduce.1
  179.8 92.6 all-gather.6
  331.7 19.5 reduce-scatter.3
